TPU v7x, 512 devices: a whole 4x8x8 slice. The times are simulated.
512 devices in a mesh: view: 8 (over y_lo, core), pencil: 64 (over y_hi, z, x).
Axes of the slice: x: 4, y: 8 (y_hi: 2, y_lo: 4; y = y_hi * 4 + y_lo), z: 8, core: 2. Of those that a mesh axis runs over, the one named last changes fastest.
Arguments:
- estimate: float32 [512, 16, 512], P('pencil'), may hold values from 0.5 to 2
- views_data: float32 [8, 512, 16, 512], P('view', 'pencil'), may hold values from 0.5 to 2
- psf_long: float32 [8, 61], P('view'), may hold values from 0.05 to 1
- psf_short: float32 [8, 2, 15], P('view'), may hold values from 0.05 to 1
- detection: int32 [8, 2], P('view'), may hold values from -12 to 12, as said below
Outputs:
- updated: float32 [512, 16, 512], P('pencil')
Inputs may be any that keep to these rules, and one draw needn't show every extreme that they name: `detection`: column 0 is 0 or 1; column 1 lies between -12 and 12, and some view has offset 12 and another -12.
All inputs are finite; a program needn't handle non-finite values.
Results may differ from a plain program's by a relative error of at most 0.0003.
Values sent between devices are 32-bit elements; how exact they have to be, the bound alone decides.
A program may use at most 64 MiB of HBM per device.

v0:
```python
import jax
import jax.numpy as jnp
from jax import lax
from jax.sharding import PartitionSpec as P


def merged(value, axis, join):
    pieces = lax.all_gather(value, axis)
    head = pieces[0]
    tail = pieces[1:]
    running, _ = lax.scan(lambda running, slab: (join(running, slab), None), head, tail)
    return running


def banded(taps, length, shift):
    count = taps.shape[0]
    radius = (count - 1) // 2
    rows = jnp.arange(length, dtype=jnp.int32)[:, None]
    cols = jnp.arange(length, dtype=jnp.int32)[None, :]
    offset = cols - rows + radius - shift
    valid = (offset >= 0) & (offset < count)
    return jnp.where(
        valid, jnp.take(taps, jnp.clip(offset, 0, count - 1)), jnp.zeros((), taps.dtype)
    )


def multiply_pair(first, second):
    return first * second


def per_device(estimate, views_data, psf_long, psf_short, detection):
    high = lax.Precision.HIGHEST
    long_taps = psf_long[0] / jnp.sum(psf_long[0])
    short_taps = psf_short[0] / jnp.sum(psf_short[0], axis=-1, keepdims=True)
    margin = (long_taps.shape[0] - short_taps.shape[1]) // 2
    padded = jnp.pad(short_taps, ((0, 0), (margin, margin)))
    axis_bit = detection[0, 0]
    offset_value = detection[0, 1]
    zero = jnp.zeros((), jnp.int32)
    first = jnp.where(axis_bit == 0, long_taps, padded[0])
    third = jnp.where(axis_bit == 0, padded[0], long_taps)
    first_shift = jnp.where(axis_bit == 0, offset_value, zero)
    third_shift = jnp.where(axis_bit == 0, zero, offset_value)
    x_matrix = banded(first, views_data.shape[3], first_shift)
    y_matrix = banded(padded[1], estimate.shape[1], zero)
    z_matrix = banded(third, estimate.shape[2], third_shift)
    field = jnp.einsum("abj,ij->abi", estimate, z_matrix, precision=high)
    field = jnp.einsum("ajc,ij->aic", field, y_matrix, precision=high)
    blurred = jnp.einsum(
        "jbc,ij->cbi",
        lax.all_to_all(field, "pencil", split_axis=2, concat_axis=0, tiled=True),
        x_matrix,
        precision=high,
    )
    ratio = views_data[0] / blurred
    back = jnp.einsum("abj,ji->abi", ratio, x_matrix, precision=high)
    back = jnp.einsum(
        "jbc,ji->cbi",
        lax.all_to_all(back, "pencil", split_axis=2, concat_axis=0, tiled=True),
        z_matrix,
        precision=high,
    )
    correction = jnp.einsum("ajc,ji->aic", back, y_matrix, precision=high)
    factor = merged(correction, "view", multiply_pair)
    updated = estimate * factor
    return updated


def solution(mesh):
    return jax.shard_map(
        per_device,
        mesh=mesh,
        in_specs=(
            P("pencil", None, None),
            P("view", "pencil", None, None),
            P("view", None),
            P("view", None, None),
            P("view", None),
        ),
        out_specs=P("pencil", None, None),
        check_vma=False,
    )
```

profile of v0, /device:TPU:1, one launch (start us, length us, event | category | flops | bytes accessed | tf_op | source)
XLA Modules:
  0.0 223.5 jit_solution(10596072240556663319)
XLA Ops:
  6.5 1.4 fusion.167
  7.9 0.8 reduce_sum.18
  8.7 0.7 bitcast_divide_fusion
  9.4 1.3 reduce_sum.19
  11.4 1.4 fusion.162
  12.8 0.1 fusion.161
  12.9 0.7 fusion.170
  13.6 0.7 fusion.169
  14.3 0.7 fusion.168
  15.0 0.6 fusion.171
  15.7 0.1 reshape.197
  15.8 1.9 gather_fusion
  17.7 0.1 reshape.196
  18.4 42.8 %select_select_fusion.1 = f32[512,512]{1,0:T(8,128)S(1)} fusion(f32[]{:T(128)} %bitcast.67, f32[]{:T(128)} %bitcast.66, f32[]{:T(128)} %bitcast.65, f32[]{:T(128)} %bitcast.64, f32[]{:T(128)} %bitcast.63, f32[]{:T(128)} %bitcast.62, f32[]{:T(128)} %bitcast.61, f32[]{:T(128)} %bitcast.60, f32[]{:T(128)} %bitcast.59, f32[]{:T(128)} %bitcast.58, f32[]{:T(128)} %bitcast.57, ...), kind=kLoop, calls=%fused_computation.20 | loop fusion | flops 35389440 | bytes 1048824 | tf_op jit(solution)/shard_map/jit(_where)/select_n | solution.py:22
  61.2 1.2 convolution_bitcast_fusion.2
  62.4 0.4 convolution_bitcast_fusion.1
  62.8 0.7 copy.12
  63.6 1.5 reshape.342
  65.0 19.6 %all-to-all-start = ((f32[64,1,1024]{2,1,0:T(1,128)}), f32[64,1,1024]{2,1,0:T(1,128)S(1)}, u32[]{:S(2)}, u32[]{:S(2)}) async-start(f32[64,1,1024]{2,1,0:T(1,128)} %reshape.342), calls=%async_computation | async-start | bytes 524288 | tf_op jit(solution)/shard_map/all_to_all | solution.py:51
  84.6 0.2 all-gather.3.cloned.1.call-start
  84.8 0.7 fusion.164
  85.6 0.7 fusion.163
  86.3 0.7 fusion.165
  87.0 0.7 fusion.166
  88.3 42.8 %select_select_fusion = f32[512,512]{1,0:T(8,128)S(1)} fusion(f32[]{:T(128)} %bitcast.131, f32[]{:T(128)} %bitcast.130, f32[]{:T(128)} %bitcast.129, f32[]{:T(128)} %bitcast.128, f32[]{:T(128)} %bitcast.127, f32[]{:T(128)} %bitcast.126, f32[]{:T(128)} %bitcast.125, f32[]{:T(128)} %bitcast.124, f32[]{:T(128)} %bitcast.123, f32[]{:T(128)} %bitcast.122, ...), kind=kLoop, calls=%fused_computation.19 | loop fusion | flops 35389440 | bytes 1048824 | tf_op jit(solution)/shard_map/jit(_where)/select_n | solution.py:22
  131.1 0.5 broadcast.818
  131.6 1.3 reduce.2
  132.9 2.1 reshape.343
  135.0 2.1 copy.14
  137.1 3.6 %fusion.10 = f32[8,16,512]{2,1,0:T(8,128)S(1)} fusion(f32[512,16,8]{1,2,0:T(8,128)S(1)} %bitcast.186, f32[512,512]{1,0:T(8,128)S(1)} %select_select_fusion, f32[1,8,16,512]{3,2,1,0:T(8,128)S(1)} %copy-done.2), kind=kOutput, calls=%fused_computation.13 | convolution fusion | flops 402718720 | bytes 1835008 | tf_op jit(solution)/shard_map/jbc,ij->cbi/dot_general | solution.py:49
  140.7 0.7 fusion.13
  141.5 0.7 copy.16
  142.2 1.0 reshape.344
  143.2 28.5 %all_to_all.36 = f32[64,1,1024]{2,1,0:T(1,128)S(1)} all-to-all(f32[64,1,1024]{2,1,0:T(1,128)S(1)} %reshape.344), channel_id=1, replica_groups=mesh['view'=8,'pencil'=64] {'pencil'}, dimensions={0} | all-to-all | bytes 524288 | tf_op jit(solution)/shard_map/all_to_all | solution.py:59
  171.7 1.3 reduce.3
  172.9 0.7 reshape.345
  173.7 0.5 copy.18
  174.1 3.6 %fusion.7 = f32[8,16,512]{2,1,0:T(8,128)S(1)} fusion(f32[512,16,8]{1,2,0:T(8,128)S(1)} %bitcast.185, f32[512,512]{1,0:T(8,128)S(1)} %select_select_fusion.1), kind=kOutput, calls=%fused_computation.9 | convolution fusion | flops 402653184 | bytes 1572864 | tf_op jit(solution)/shard_map/jbc,ji->cbi/dot_general | solution.py:57
  177.7 1.1 convolution_bitcast_fusion
  178.9 34.3 %all-gather.3.cloned.1.call-done = f32[64,16,512]{2,1,0:T(8,128)} async-done(((f32[8,16,512]{2,1,0:T(8,128)}), f32[64,16,512]{2,1,0:T(8,128)}) %all-gather.3.cloned.1.call-update) | async-done | bytes 2097168 | tf_op jit(solution)/shard_map/all_gather | solution.py:8
  213.2 1.7 slice.276
  214.9 0.6 while.10
  215.0 0.1 bitcast_multiply_fusion.2
  215.0 0.1 bitcast_multiply_fusion.2
  215.2 0.1 bitcast_multiply_fusion.2
  215.3 0.1 bitcast_multiply_fusion.2
  215.6 0.3 copy-done.1
  215.9 0.7 mul.6
  (14 shorter events, 0.2 us)
Async XLA Ops:
  15.8 45.4 %copy-start = (f32[8,16,512]{2,1,0:T(8,128)S(1)}, f32[8,16,512]{2,1,0:T(8,128)}, u32[]{:S(2)}) copy-start(f32[8,16,512]{2,1,0:T(8,128)} %param.9) | copy-start | bytes 786436
  65.0 66.1 %all-to-all-start = ((f32[64,1,1024]{2,1,0:T(1,128)}), f32[64,1,1024]{2,1,0:T(1,128)S(1)}, u32[]{:S(2)}, u32[]{:S(2)}) async-start(f32[64,1,1024]{2,1,0:T(1,128)} %reshape.342), calls=%async_computation | async-start | bytes 524288 | tf_op jit(solution)/shard_map/all_to_all | solution.py:51
  84.6 128.6 %all-gather.3.cloned.1.call-start = ((), (), s32[]{:S(2)}) async-start(), calls=%async_computation.2 | async-start | bytes 2359296 | tf_op jit(solution)/shard_map/all_gather | solution.py:8
  135.0 2.1 copy-start.2
  213.2 1.7 slice-start
  214.9 1.0 copy-start.1
Sparse Core Ops, SparseCore 0:
  179.0 34.1 all-gather.2
where the time goes:
time: 226 us; the launch traced here: 223 us
  other arithmetic  93.6 us (41%)
  waiting for transfers between devices  34.3 us (15%)
  blocking collectives  28.5 us (13%)
  local copies, waits for them, and re-layouts  20.8 us (9%)
  starting transfers between devices  19.8 us (9%)
  between operations  15.5 us (7%)
  matrix products  10.7 us (5%)
    select_n x2, other arithmetic, banded(): jnp.where(valid, jnp.take(taps, jnp.clip(offset, 0, count - 1)), jnp.zero...  85.6 us
    all_gather x1, waiting for transfers between devices, merged(): pieces = lax.all_gather(value, axis)  34.3 us
    all_to_all x1, blocking collectives, per_device(): lax.all_to_all(back, 'pencil', split_axis=2, concat_axis=0, tiled=True)  28.5 us
    all_to_all x1, starting transfers between devices, per_device(): lax.all_to_all(field, 'pencil', split_axis=2, concat_axis=0, tiled=True)  19.6 us
    gather x10, local copies, waits for them, and re-layouts, banded(): jnp.take(taps, jnp.clip(offset, 0, count - 1))  7.61 us
    unnamed x10, local copies, waits for them, and re-layouts  5.52 us
  transfers between devices with their start and end apart: 2, of which 1 were waited for; matrix products, arithmetic and copies ran while one was open for 20% of the time, Pallas kernels for 0%

commit v1 on v0

v1 whole, which is shorter than its diff:
```python
import functools

import jax
import jax.numpy as jnp
from jax import lax
from jax.experimental import pallas as pl
from jax.experimental.pallas import tpu as pltpu
from jax.sharding import PartitionSpec as P

F32 = jnp.float32
BF16 = jnp.bfloat16
MESH = pl.DeviceIdType.MESH

VIEWS = 8
PENCILS = 64
TILE = 8
N = 512
L = 128
YDIM = 16

NN = (((1,), (0,)), ((), ()))
NT = (((1,), (1,)), ((), ()))

OFFSETS = sorted(
    ((a, b, c) for a in range(2) for b in range(8) for c in range(4) if a + b + c),
    key=lambda o: (-(4 * o[0] + min(o[1], 8 - o[1]) + min(o[2], 4 - o[2])), o),
)


def split(a):
    hi = a.astype(BF16)
    lo = (a - hi.astype(F32)).astype(BF16)
    return hi, lo


def dot3(a, b, dims):
    ah, al = a
    bh, bl = b
    dot = functools.partial(
        lax.dot_general, dimension_numbers=dims, preferred_element_type=F32
    )
    return dot(ah, bh) + (dot(ah, bl) + dot(al, bh))


def roll(x, shift, axis):
    return pltpu.roll(x, shift % x.shape[axis], axis)


def shifted(row, amount):
    for bit in range(5):
        flag = ((amount >> bit) & 1) == 1
        row = jnp.where(flag, roll(row, 1 << bit, 1), row)
    return row


def staircase(row, start):
    eight = jnp.broadcast_to(row, (8, row.shape[1]))
    eight = pltpu.roll(eight, 0, 1, stride=1, stride_axis=0)
    return jnp.concatenate([roll(eight, start + 8 * k, 1) for k in range(L // 8)], axis=0)


def band_blocks(row, amount):
    row = shifted(row, amount + 12)
    wide = jnp.concatenate([row, jnp.zeros((1, 2 * L), F32)], axis=1)
    return staircase(wide, 86)


def y_block(row):
    full = staircase(row, 121)
    rows = lax.broadcasted_iota(jnp.int32, (L, L), 0) // YDIM
    cols = lax.broadcasted_iota(jnp.int32, (L, L), 1) // YDIM
    return jnp.where(rows == cols, full, 0.0)


def swap_slab(x):
    x = x.reshape(PENCILS, TILE, L)
    sub = lax.broadcasted_iota(jnp.int32, x.shape, 1)
    lane = lax.broadcasted_iota(jnp.int32, x.shape, 2) // YDIM
    for bit in (4, 2, 1):
        s_bit = (sub // bit) % 2
        same = s_bit == (lane // bit) % 2
        up = roll(roll(x, -bit, 1), YDIM * bit, 2)
        down = up if bit == 4 else roll(roll(x, bit, 1), -YDIM * bit, 2)
        x = jnp.where(same, x, jnp.where(s_bit == 0, up, down))
    return x.reshape(PENCILS * TILE, L)


def taps(long_ref, short_ref, detect_ref, rows):
    rows[...] = jnp.zeros_like(rows)
    rows[0:1, 0 : long_ref.shape[1]] = long_ref[...]
    rows[1:3, 0 : short_ref.shape[2]] = short_ref[0]
    value = rows[...]
    value = value / jnp.maximum(jnp.sum(value, axis=1, keepdims=True), 1e-30)
    along, across, second = value[0:1], roll(value[1:2], 23, 1), value[2:3]
    is_first = detect_ref[0, 0] == 0
    offset = detect_ref[0, 1]
    first = jnp.where(is_first, along, across)
    third = jnp.where(is_first, across, along)
    return (
        (first, jnp.where(is_first, offset, 0)),
        second,
        (third, jnp.where(is_first, 0, offset)),
    )


def store_pair(ref, rows, cols, value):
    hi, lo = split(value)
    ref[0, rows, cols] = hi
    ref[1, rows, cols] = lo


def fill_rows(ref, blocks):
    zero = jnp.zeros((L, L), BF16)
    for part in range(2):
        ref[part, 0:L, 3 * L : 4 * L] = zero
        ref[part, L : 2 * L, 0:L] = zero
    store_pair(ref, slice(0, L), slice(0, 3 * L), blocks)
    store_pair(ref, slice(L, 2 * L), slice(L, 4 * L), blocks)


def fill_cols(ref, blocks):
    zero = jnp.zeros((L, L), BF16)
    left, here, right = (blocks[:, k * L : (k + 1) * L] for k in range(3))
    for part in range(2):
        ref[part, 0:L, L : 2 * L] = zero
        ref[part, 3 * L : 4 * L, 0:L] = zero
    for col in range(2):
        for row, value in enumerate((right, here, left)):
            store_pair(
                ref,
                slice((row + col) * L, (row + col + 1) * L),
                slice(col * L, (col + 1) * L),
                value,
            )


HALVES = ((0, slice(L, 4 * L), slice(0, 3 * L)), (1, slice(0, 3 * L), slice(L, 4 * L)))


def kernel(
    est_ref, views_ref, long_ref, short_ref, detect_ref, out_ref,
    rows, zrow, zcol, xrow, xtrow, ymat, views_t,
    send1, recv1, send2, recv2, corr, gathered,
    ssem, rsem,
):
    v = lax.axis_index("view")
    q = lax.axis_index("pencil")
    x, z, yh = q % 4, (q // 4) % 8, q // 32

    def pencil(off):
        a, b, c = off
        return (((yh + a) % 2) * 8 + (z + b) % 8) * 4 + (x + c) % 4

    barrier = pltpu.get_barrier_semaphore()
    for off in OFFSETS:
        pl.semaphore_signal(barrier, inc=1, device_id=(v, pencil(off)), device_id_type=MESH)
    for k in range(1, VIEWS):
        pl.semaphore_signal(barrier, inc=1, device_id=((v + k) % VIEWS, q), device_id_type=MESH)

    (first, first_shift), second, (third, third_shift) = taps(
        long_ref, short_ref, detect_ref, rows
    )
    yb = y_block(second)
    store_pair(ymat, slice(0, L), slice(0, L), yb)
    zb = band_blocks(third, third_shift)
    fill_rows(zrow, zb)

    est = est_ref[...]
    field = dot3(split(yb), split(est), NN)
    fh, fl = split(field)
    for half, cols, window in HALVES:
        send1[half * 256 : (half + 1) * 256, :] = dot3(
            (zrow[0, :, cols], zrow[1, :, cols]), (fh[:, window], fl[:, window]), NT
        )

    pl.semaphore_wait(barrier, PENCILS - 1 + VIEWS - 1)

    def exchange(src, dst, k):
        mine = pl.ds(pl.multiple_of(q * TILE, TILE), TILE)
        for off in OFFSETS:
            peer = pencil(off)
            pltpu.make_async_remote_copy(
                src_ref=src.at[pl.ds(pl.multiple_of(peer * TILE, TILE), TILE), :],
                dst_ref=dst.at[mine, :],
                send_sem=ssem.at[k],
                recv_sem=rsem.at[k],
                device_id=(v, peer),
                device_id_type=MESH,
            ).start()
        dst[mine, :] = src[mine, :]

    def arrived(src, dst, k, count):
        span = pl.ds(0, count)
        both = pltpu.make_async_copy(src.at[span], dst.at[span], rsem.at[k])
        both.wait()
        pltpu.make_async_copy(src.at[span], dst.at[span], ssem.at[k]).wait()

    exchange(send1, recv1, 0)
    xb = band_blocks(first, first_shift)
    fill_rows(xrow, xb)
    fill_rows(
        xtrow,
        jnp.concatenate([xb[:, k * L : (k + 1) * L].T for k in (2, 1, 0)], axis=1),
    )
    fill_cols(zcol, zb)
    ytb = split(yb.T)
    views_t[...] = views_ref[...].T
    arrived(send1, recv1, 0, (PENCILS - 1) * TILE)

    gh, gl = split(swap_slab(recv1[...]))
    ratio = []
    for half, cols, window in HALVES:
        blurred = dot3(
            (xrow[0, :, cols], xrow[1, :, cols]), (gh[window], gl[window]), NN
        )
        ratio.append(views_t[half * 256 : (half + 1) * 256, :] / blurred)
    rh, rl = split(jnp.concatenate(ratio, axis=0))
    back = jnp.concatenate(
        [
            dot3((xtrow[0, :, cols], xtrow[1, :, cols]), (rh[window], rl[window]), NN)
            for _, cols, window in HALVES
        ],
        axis=0,
    )
    send2[...] = swap_slab(back)
    exchange(send2, recv2, 1)
    arrived(send2, recv2, 1, (PENCILS - 1) * TILE)

    bh, bl = split(recv2[...].T)
    whole = jnp.concatenate(
        [
            dot3((bh[:, window], bl[:, window]), (zcol[0, rows_, :], zcol[1, rows_, :]), NN)
            for _, rows_, window in HALVES
        ],
        axis=1,
    )
    corr[...] = dot3(ytb, split(whole), NN)

    slab = pl.ds(pl.multiple_of(v * YDIM, YDIM), YDIM)
    for k in range(1, VIEWS):
        peer = (v + k) % VIEWS
        pltpu.make_async_remote_copy(
            src_ref=corr.at[pl.ds(pl.multiple_of(peer * YDIM, YDIM), YDIM), :],
            dst_ref=gathered.at[slab, :],
            send_sem=ssem.at[2],
            recv_sem=rsem.at[2],
            device_id=(peer, q),
            device_id_type=MESH,
        ).start()
    gathered[slab, :] = corr[slab, :]
    arrived(corr, gathered, 2, (VIEWS - 1) * YDIM)
    factor = gathered[0:YDIM, :]
    for k in range(1, VIEWS):
        factor = factor * gathered[k * YDIM : (k + 1) * YDIM, :]
    out_ref[slab, :] = est_ref[slab, :] * factor
    for k in range(1, VIEWS):
        pltpu.make_async_remote_copy(
            src_ref=out_ref.at[slab, :],
            dst_ref=out_ref.at[slab, :],
            send_sem=ssem.at[3],
            recv_sem=rsem.at[3],
            device_id=((v + k) % VIEWS, q),
            device_id_type=MESH,
        ).start()
    arrived(out_ref, out_ref, 3, (VIEWS - 1) * YDIM)


def per_device(estimate, views_data, psf_long, psf_short, detection):
    vmem = pl.BlockSpec(memory_space=pltpu.VMEM)
    flat = pl.pallas_call(
        kernel,
        out_shape=jax.ShapeDtypeStruct((L, N), F32),
        in_specs=[vmem, vmem, vmem, vmem, pl.BlockSpec(memory_space=pltpu.SMEM)],
        out_specs=vmem,
        scratch_shapes=[
            pltpu.VMEM((8, L), F32),
            pltpu.VMEM((2, 2 * L, 4 * L), BF16),
            pltpu.VMEM((2, 4 * L, 2 * L), BF16),
            pltpu.VMEM((2, 2 * L, 4 * L), BF16),
            pltpu.VMEM((2, 2 * L, 4 * L), BF16),
            pltpu.VMEM((2, L, L), BF16),
            pltpu.VMEM((N, L), F32),
            pltpu.VMEM((N, L), F32),
            pltpu.VMEM((N, L), F32),
            pltpu.VMEM((N, L), F32),
            pltpu.VMEM((N, L), F32),
            pltpu.VMEM((L, N), F32),
            pltpu.VMEM((L, N), F32),
            pltpu.SemaphoreType.DMA((4,)),
            pltpu.SemaphoreType.DMA((4,)),
        ],
        compiler_params=pltpu.CompilerParams(collective_id=0, has_side_effects=True),
    )(
        estimate.reshape(L, N),
        views_data.reshape(L, N),
        psf_long,
        psf_short,
        detection,
    )
    return flat.reshape(estimate.shape)


def solution(mesh):
    return jax.shard_map(
        per_device,
        mesh=mesh,
        in_specs=(
            P("pencil", None, None),
            P("view", "pencil", None, None),
            P("view", None),
            P("view", None, None),
            P("view", None),
        ),
        out_specs=P("pencil", None, None),
        check_vma=False,
    )
```

time: 226 us -> 56.2 us (0.25); the launches traced: 223 us -> 56.1 us
  other arithmetic: 93.6 us -> 0 us
  Pallas kernels: 0 us -> 54.4 us
  waiting for transfers between devices: 34.3 us -> 0 us
  blocking collectives: 28.5 us -> 0 us
  starting transfers between devices: 19.8 us -> 0 us
  local copies, waits for them, and re-layouts: 20.8 us -> 1.67 us
  between operations: 15.5 us -> 0.01 us
  matrix products: 10.7 us -> 0 us
    select_n x5 -> x0, other arithmetic: 87.1 us -> none  [the longest x2 85.6 us: banded(): jnp.where(valid, jnp.take(taps, jnp.clip(offset, 0, count - 1)), jnp.zero...]
    pallas_call x0 -> x1, Pallas kernels: none -> 54.4 us  [per_device(): pl.pallas_call(kernel, out_shape=jax.ShapeDtypeStruct((L, N), F32), in_sp...]
    all_gather x1 -> x0, waiting for transfers between devices: 34.3 us -> none  [merged(): pieces = lax.all_gather(value, axis)]
    all_to_all x1 -> x0, blocking collectives: 28.5 us -> none  [per_device(): lax.all_to_all(back, 'pencil', split_axis=2, concat_axis=0, tiled=True)]
    all_to_all x1 -> x0, starting transfers between devices: 19.6 us -> none  [per_device(): lax.all_to_all(field, 'pencil', split_axis=2, concat_axis=0, tiled=True)]
    dot_general x6 -> x0, matrix products: 10.7 us -> none  [the longest x1 3.65 us: per_device(): jnp.einsum('jbc,ij->cbi', lax.all_to_all(field, 'pencil', split_axis=2, c...]
    gather x10 -> x0, local copies, waits for them, and re-layouts: 7.61 us -> none  [banded(): jnp.take(taps, jnp.clip(offset, 0, count - 1))]
    unnamed x10 -> x1, local copies, waits for them, and re-layouts: 5.52 us -> 1.67 us
  transfers between devices with their start and end apart: 2 -> 0, of which waited for: 1 -> 0; matrix products, arithmetic and copies ran while one was open for 20% -> 0% of each run, Pallas kernels for 0% -> 0%
where the time goes in v1:
time: 56.2 us; the launch traced here: 56.1 us
  Pallas kernels  54.4 us (97%)
  local copies, waits for them, and re-layouts  1.67 us (3%)
    pallas_call x1, Pallas kernels, per_device(): pl.pallas_call(kernel, out_shape=jax.ShapeDtypeStruct((L, N), F32), in_sp...  54.4 us
    unnamed x1, local copies, waits for them, and re-layouts  1.67 us

profile of v1, /device:TPU:1, one launch (start us, length us, event | category | flops | bytes accessed | tf_op | source)
XLA Modules:
  0.0 56.1 jit_solution(2677275962330345321)
XLA Ops:
  0.0 54.4 %shard_map.55 = f32[128,512]{1,0:T(8,128)} custom-call(f32[128,512]{1,0:T(8,128)} %bitcast.4, f32[128,512]{1,0:T(8,128)} %bitcast.5, f32[1,61]{1,0:T(1,128)} %long_ref.1, f32[1,2,15]{2,1,0:T(2,128)} %short_ref.1, s32[1,2]{1,0:T(1,128)} %detect_ref.1), custom_call_target="tpu_custom_call" | custom-call | tf_op jit(solution)/shard_map/pallas_call | solution.py:270
  54.4 1.7 %copy.7 = f32[8,16,512]{2,1,0:T(8,128)} copy(f32[8,16,512]{2,1,0:T(8,128)} %bitcast.3) | data formatting | bytes 524288

commit v2 on v1

--- a/solution.py
+++ b/solution.py
@@ -12,6 +12,7 @@
 MESH = pl.DeviceIdType.MESH
 
 VIEWS = 8
+CHIPS = 4
 PENCILS = 64
 TILE = 8
 N = 512
@@ -138,10 +139,12 @@
 
 
 def kernel(
-    est_ref, views_ref, long_ref, short_ref, detect_ref, out_ref,
-    rows, zrow, zcol, xrow, xtrow, ymat, views_t,
-    send1, recv1, send2, recv2, corr, gathered,
-    ssem, rsem,
+    est_hbm, views_hbm, long_hbm, short_hbm, detect_hbm, out_ref,
+    est_ref, views_ref, long_ref, short_ref, detect_ref,
+    rows, zrow, zcol, xrow, xtrow, views_t,
+    send1, recv1, send2, recv2, corr, pair, part, merged,
+    isem, ssem, rsem, pair_ssem, pair_rsem, part_ssem, part_rsem,
+    chip_ssem, chip_rsem, core_ssem, core_rsem,
 ):
     v = lax.axis_index("view")
     q = lax.axis_index("pencil")
@@ -154,26 +157,48 @@
     barrier = pltpu.get_barrier_semaphore()
     for off in OFFSETS:
         pl.semaphore_signal(barrier, inc=1, device_id=(v, pencil(off)), device_id_type=MESH)
-    for k in range(1, VIEWS):
-        pl.semaphore_signal(barrier, inc=1, device_id=((v + k) % VIEWS, q), device_id_type=MESH)
+    core, chip = v % 2, v // 2
+    partner = (chip * 2 + (1 - core), q)
+    chips = [(3 - chip) % CHIPS, (chip + 2) % CHIPS, (5 - chip) % CHIPS]
+    pl.semaphore_signal(barrier, inc=1, device_id=partner, device_id_type=MESH)
+    for other in chips:
+        pl.semaphore_signal(
+            barrier, inc=1, device_id=(other * 2 + core, q), device_id_type=MESH
+        )
+
+    loads = [
+        pltpu.make_async_copy(src, dst, isem.at[k])
+        for k, (src, dst) in enumerate(
+            (
+                (long_hbm, long_ref),
+                (short_hbm, short_ref),
+                (detect_hbm, detect_ref),
+                (est_hbm, est_ref),
+                (views_hbm, views_ref),
+            )
+        )
+    ]
+    for load in loads:
+        load.start()
+    for load in loads[:3]:
+        load.wait()
 
     (first, first_shift), second, (third, third_shift) = taps(
         long_ref, short_ref, detect_ref, rows
     )
     yb = y_block(second)
-    store_pair(ymat, slice(0, L), slice(0, L), yb)
     zb = band_blocks(third, third_shift)
     fill_rows(zrow, zb)
 
-    est = est_ref[...]
-    field = dot3(split(yb), split(est), NN)
+    loads[3].wait()
+    field = dot3(split(yb), split(est_ref[...]), NN)
     fh, fl = split(field)
     for half, cols, window in HALVES:
         send1[half * 256 : (half + 1) * 256, :] = dot3(
             (zrow[0, :, cols], zrow[1, :, cols]), (fh[:, window], fl[:, window]), NT
         )
 
-    pl.semaphore_wait(barrier, PENCILS - 1 + VIEWS - 1)
+    pl.semaphore_wait(barrier, PENCILS - 1 + CHIPS)
 
     def exchange(src, dst, k):
         mine = pl.ds(pl.multiple_of(q * TILE, TILE), TILE)
@@ -204,6 +229,7 @@
     )
     fill_cols(zcol, zb)
     ytb = split(yb.T)
+    loads[4].wait()
     views_t[...] = views_ref[...].T
     arrived(send1, recv1, 0, (PENCILS - 1) * TILE)
 
@@ -236,60 +262,117 @@
     )
     corr[...] = dot3(ytb, split(whole), NN)
 
-    slab = pl.ds(pl.multiple_of(v * YDIM, YDIM), YDIM)
-    for k in range(1, VIEWS):
-        peer = (v + k) % VIEWS
-        pltpu.make_async_remote_copy(
-            src_ref=corr.at[pl.ds(pl.multiple_of(peer * YDIM, YDIM), YDIM), :],
-            dst_ref=gathered.at[slab, :],
-            send_sem=ssem.at[2],
-            recv_sem=rsem.at[2],
-            device_id=(peer, q),
+    def quarter(c, b):
+        return pl.ds(pl.multiple_of((c * CHIPS + b) * YDIM, YDIM), YDIM)
+
+    halves = []
+    for k, b in enumerate(chips + [chip]):
+        send = pltpu.make_async_remote_copy(
+            src_ref=corr.at[quarter(1 - core, b), :],
+            dst_ref=pair.at[b],
+            send_sem=pair_ssem.at[k],
+            recv_sem=pair_rsem.at[k],
+            device_id=partner,
             device_id_type=MESH,
-        ).start()
-    gathered[slab, :] = corr[slab, :]
-    arrived(corr, gathered, 2, (VIEWS - 1) * YDIM)
-    factor = gathered[0:YDIM, :]
-    for k in range(1, VIEWS):
-        factor = factor * gathered[k * YDIM : (k + 1) * YDIM, :]
-    out_ref[slab, :] = est_ref[slab, :] * factor
-    for k in range(1, VIEWS):
-        pltpu.make_async_remote_copy(
-            src_ref=out_ref.at[slab, :],
-            dst_ref=out_ref.at[slab, :],
-            send_sem=ssem.at[3],
-            recv_sem=rsem.at[3],
-            device_id=((v + k) % VIEWS, q),
+        )
+        send.start()
+        halves.append(send)
+    quarters = []
+    for k, b in enumerate(chips + [chip]):
+        halves[k].wait_recv()
+        pair[b] = pair[b] * corr[quarter(core, b), :]
+        if k < CHIPS - 1:
+            send = pltpu.make_async_remote_copy(
+                src_ref=pair.at[b],
+                dst_ref=part.at[k],
+                send_sem=part_ssem.at[k],
+                recv_sem=part_rsem.at[k],
+                device_id=(b * 2 + core, q),
+                device_id_type=MESH,
+            )
+            send.start()
+            quarters.append(send)
+    factor = pair[chip]
+    for k, send in enumerate(quarters):
+        send.wait_recv()
+    for k in range(CHIPS - 1):
+        factor = factor * part[k]
+    mine = quarter(core, chip)
+    merged[mine, :] = factor
+
+    gathers = []
+    for k, b in enumerate(chips):
+        send = pltpu.make_async_remote_copy(
+            src_ref=merged.at[mine, :],
+            dst_ref=merged.at[mine, :],
+            send_sem=chip_ssem.at[k],
+            recv_sem=chip_rsem.at[k],
+            device_id=(b * 2 + core, q),
             device_id_type=MESH,
-        ).start()
-    arrived(out_ref, out_ref, 3, (VIEWS - 1) * YDIM)
+        )
+        send.start()
+        gathers.append(send)
+
+    def forward(k, where):
+        send = pltpu.make_async_remote_copy(
+            src_ref=merged.at[where, :],
+            dst_ref=merged.at[where, :],
+            send_sem=core_ssem.at[k],
+            recv_sem=core_rsem.at[k],
+            device_id=partner,
+            device_id_type=MESH,
+        )
+        send.start()
+        return send
+
+    relays = [forward(CHIPS - 1, mine)]
+    for k in (2, 1, 0):
+        gathers[k].wait_recv()
+        relays.append(forward(k, quarter(core, chips[k])))
+    for send in halves + quarters + gathers:
+        send.wait_send()
+    for send in relays:
+        send.wait()
+    final = pltpu.make_async_copy(merged, out_ref, isem.at[0])
+    final.start()
+    final.wait()
 
 
 def per_device(estimate, views_data, psf_long, psf_short, detection):
-    vmem = pl.BlockSpec(memory_space=pltpu.VMEM)
-    flat = pl.pallas_call(
+    raw = pl.BlockSpec(memory_space=pl.ANY)
+    dma = pltpu.SemaphoreType.DMA
+    factor = pl.pallas_call(
         kernel,
         out_shape=jax.ShapeDtypeStruct((L, N), F32),
-        in_specs=[vmem, vmem, vmem, vmem, pl.BlockSpec(memory_space=pltpu.SMEM)],
-        out_specs=vmem,
+        in_specs=[raw] * 5,
+        out_specs=raw,
         scratch_shapes=[
+            pltpu.VMEM((L, N), F32),
+            pltpu.VMEM((L, N), F32),
+            pltpu.VMEM(psf_long.shape, F32),
+            pltpu.VMEM(psf_short.shape, F32),
+            pltpu.SMEM(detection.shape, jnp.int32),
             pltpu.VMEM((8, L), F32),
             pltpu.VMEM((2, 2 * L, 4 * L), BF16),
             pltpu.VMEM((2, 4 * L, 2 * L), BF16),
             pltpu.VMEM((2, 2 * L, 4 * L), BF16),
             pltpu.VMEM((2, 2 * L, 4 * L), BF16),
-            pltpu.VMEM((2, L, L), BF16),
             pltpu.VMEM((N, L), F32),
             pltpu.VMEM((N, L), F32),
             pltpu.VMEM((N, L), F32),
             pltpu.VMEM((N, L), F32),
             pltpu.VMEM((N, L), F32),
             pltpu.VMEM((L, N), F32),
+            pltpu.VMEM((CHIPS, YDIM, N), F32),
+            pltpu.VMEM((CHIPS - 1, YDIM, N), F32),
             pltpu.VMEM((L, N), F32),
-            pltpu.SemaphoreType.DMA((4,)),
-            pltpu.SemaphoreType.DMA((4,)),
+            dma((5,)), dma((2,)), dma((2,)),
+            dma((CHIPS,)), dma((CHIPS,)), dma((CHIPS - 1,)), dma((CHIPS - 1,)),
+            dma((CHIPS - 1,)), dma((CHIPS - 1,)), dma((CHIPS,)), dma((CHIPS,)),
         ],
-        compiler_params=pltpu.CompilerParams(collective_id=0, has_side_effects=True),
+        compiler_params=pltpu.CompilerParams(
+            collective_id=0, has_side_effects=True
+        ),
     )(
         estimate.reshape(L, N),
         views_data.reshape(L, N),
@@ -297,7 +380,7 @@
         psf_short,
         detection,
     )
-    return flat.reshape(estimate.shape)
+    return estimate * factor.reshape(estimate.shape)
 
 
 def solution(mesh):

time: 56.2 us -> 55.6 us (0.989)
  other arithmetic: 0 us -> 1.69 us
  local copies, waits for them, and re-layouts: 1.67 us -> 0.01 us
  Pallas kernels: 54.4 us -> 53.7 us
    mul x0 -> x1, other arithmetic: none -> 1.69 us  [per_device(): return estimate * factor.reshape(estimate.shape)]
    unnamed x1 -> x2, local copies, waits for them, and re-layouts: 1.67 us -> 0.01 us
    pallas_call x1, Pallas kernels: 54.4 us -> 53.7 us  [per_device(): pl.pallas_call(kernel, out_shape=jax.ShapeDtypeStruct((L, N), F32), in_sp...]
where the time goes in v2:
time: 55.6 us; the launch traced here: 55.4 us
  Pallas kernels  53.7 us (97%)
  other arithmetic  1.69 us (3%)
    pallas_call x1, Pallas kernels, per_device(): pl.pallas_call(kernel, out_shape=jax.ShapeDtypeStruct((L, N), F32), in_sp...  53.7 us
    mul x1, other arithmetic, per_device(): return estimate * factor.reshape(estimate.shape)  1.69 us

profile of v2, /device:TPU:1, one launch (start us, length us, event | category | flops | bytes accessed | tf_op | source)
XLA Modules:
  0.0 55.4 jit_solution(7639401644443879873)
XLA Ops:
  0.0 0.0 copy-start
  0.0 53.7 %shard_map.55 = f32[128,512]{1,0:T(8,128)} custom-call(f32[128,512]{1,0:T(8,128)} %bitcast.3, f32[128,512]{1,0:T(8,128)} %bitcast.5, f32[1,61]{1,0:T(1,128)} %long_hbm.1, f32[1,2,15]{2,1,0:T(2,128)} %short_hbm.1, s32[1,2]{1,0:T(1,128)} %detect_hbm.1), custom_call_target="tpu_custom_call" | custom-call | tf_op jit(solution)/shard_map/pallas_call | solution.py:344
  53.7 0.0 copy-done
  53.7 1.7 %mul.3 = f32[8,16,512]{2,1,0:T(8,128)} multiply(f32[8,16,512]{2,1,0:T(8,128)S(1)} %copy-done, f32[8,16,512]{2,1,0:T(8,128)} %bitcast.4) | non-fusion elementwise | flops 65536 | bytes 786432 | tf_op jit(solution)/shard_map/mul | solution.py:383
Async XLA Ops:
  0.0 53.7 %copy-start = (f32[8,16,512]{2,1,0:T(8,128)S(1)}, f32[8,16,512]{2,1,0:T(8,128)}, u32[]{:S(2)}) copy-start(f32[8,16,512]{2,1,0:T(8,128)} %param.5) | copy-start | bytes 786436

commit v3 on v2

--- a/solution.py
+++ b/solution.py
@@ -16,6 +16,8 @@
 PENCILS = 64
 TILE = 8
 N = 512
+CHUNKS = 2
+HALF = N // CHUNKS
 L = 128
 YDIM = 16
 
@@ -142,7 +144,7 @@
     est_hbm, views_hbm, long_hbm, short_hbm, detect_hbm, out_ref,
     est_ref, views_ref, long_ref, short_ref, detect_ref,
     rows, zrow, zcol, xrow, xtrow, views_t,
-    send1, recv1, send2, recv2, corr, pair, part, merged,
+    send1, recv1, send2, recv2, corr, pair, part, final,
     isem, ssem, rsem, pair_ssem, pair_rsem, part_ssem, part_rsem,
     chip_ssem, chip_rsem, core_ssem, core_rsem,
 ):
@@ -252,90 +254,73 @@
     exchange(send2, recv2, 1)
     arrived(send2, recv2, 1, (PENCILS - 1) * TILE)
 
-    bh, bl = split(recv2[...].T)
-    whole = jnp.concatenate(
-        [
-            dot3((bh[:, window], bl[:, window]), (zcol[0, rows_, :], zcol[1, rows_, :]), NN)
-            for _, rows_, window in HALVES
-        ],
-        axis=1,
-    )
-    corr[...] = dot3(ytb, split(whole), NN)
-
     def quarter(c, b):
         return pl.ds(pl.multiple_of((c * CHIPS + b) * YDIM, YDIM), YDIM)
 
-    halves = []
-    for k, b in enumerate(chips + [chip]):
+    def remote(src, dst, sems, index, device):
         send = pltpu.make_async_remote_copy(
-            src_ref=corr.at[quarter(1 - core, b), :],
-            dst_ref=pair.at[b],
-            send_sem=pair_ssem.at[k],
-            recv_sem=pair_rsem.at[k],
-            device_id=partner,
-            device_id_type=MESH,
-        )
-        send.start()
-        halves.append(send)
-    quarters = []
-    for k, b in enumerate(chips + [chip]):
-        halves[k].wait_recv()
-        pair[b] = pair[b] * corr[quarter(core, b), :]
-        if k < CHIPS - 1:
-            send = pltpu.make_async_remote_copy(
-                src_ref=pair.at[b],
-                dst_ref=part.at[k],
-                send_sem=part_ssem.at[k],
-                recv_sem=part_rsem.at[k],
-                device_id=(b * 2 + core, q),
-                device_id_type=MESH,
-            )
-            send.start()
-            quarters.append(send)
-    factor = pair[chip]
-    for k, send in enumerate(quarters):
-        send.wait_recv()
-    for k in range(CHIPS - 1):
-        factor = factor * part[k]
-    mine = quarter(core, chip)
-    merged[mine, :] = factor
-
-    gathers = []
-    for k, b in enumerate(chips):
-        send = pltpu.make_async_remote_copy(
-            src_ref=merged.at[mine, :],
-            dst_ref=merged.at[mine, :],
-            send_sem=chip_ssem.at[k],
-            recv_sem=chip_rsem.at[k],
-            device_id=(b * 2 + core, q),
-            device_id_type=MESH,
-        )
-        send.start()
-        gathers.append(send)
-
-    def forward(k, where):
-        send = pltpu.make_async_remote_copy(
-            src_ref=merged.at[where, :],
-            dst_ref=merged.at[where, :],
-            send_sem=core_ssem.at[k],
-            recv_sem=core_rsem.at[k],
-            device_id=partner,
+            src_ref=src,
+            dst_ref=dst,
+            send_sem=sems[0].at[index],
+            recv_sem=sems[1].at[index],
+            device_id=device,
             device_id_type=MESH,
         )
         send.start()
         return send
 
-    relays = [forward(CHIPS - 1, mine)]
-    for k in (2, 1, 0):
-        gathers[k].wait_recv()
-        relays.append(forward(k, quarter(core, chips[k])))
-    for send in halves + quarters + gathers:
-        send.wait_send()
-    for send in relays:
+    order = chips + [chip]
+    same_core = [(b * 2 + core, q) for b in chips]
+    bh, bl = split(recv2[...].T)
+    halves = {}
+    for c, (_, rows_, window) in enumerate(HALVES):
+        whole = dot3(
+            (bh[:, window], bl[:, window]), (zcol[0, rows_, :], zcol[1, rows_, :]), NN
+        )
+        corr[c] = dot3(ytb, split(whole), NN)
+        for k, b in enumerate(order):
+            halves[c, k] = remote(
+                corr.at[c, quarter(1 - core, b), :], pair.at[c, b],
+                (pair_ssem, pair_rsem), c * CHIPS + k, partner,
+            )
+    quarters = {}
+    for c in range(CHUNKS):
+        for k, b in enumerate(order):
+            halves[c, k].wait_recv()
+            pair[c, b] = pair[c, b] * corr[c, quarter(core, b), :]
+            if k < CHIPS - 1:
+                quarters[c, k] = remote(
+                    pair.at[c, b], part.at[c, k],
+                    (part_ssem, part_rsem), c * CHIPS + k, same_core[k],
+                )
+    gathers, locals_, relays = {}, [], []
+    mine = quarter(core, chip)
+    for c in range(CHUNKS):
+        cols = pl.ds(c * HALF, HALF)
+        for k in range(CHIPS - 1):
+            quarters[c, k].wait_recv()
+        final[c] = (pair[c, chip] * part[c, 0]) * (part[c, 1] * part[c, 2])
+        target = out_ref.at[mine, cols]
+        for k in range(CHIPS - 1):
+            gathers[c, k] = remote(
+                final.at[c], target, (chip_ssem, chip_rsem), c * CHIPS + k, same_core[k]
+            )
+        relays.append(
+            remote(final.at[c], target, (core_ssem, core_rsem), c * CHIPS + CHIPS - 1, partner)
+        )
+        local = pltpu.make_async_copy(final.at[c], target, isem.at[c])
+        local.start()
+        locals_.append(local)
+    for c in range(CHUNKS):
+        for k in (2, 1, 0):
+            gathers[c, k].wait_recv()
+            where = out_ref.at[quarter(core, chips[k]), pl.ds(c * HALF, HALF)]
+            relays.append(remote(where, where, (core_ssem, core_rsem), c * CHIPS + k, partner))
+    for sends in (halves, quarters, gathers):
+        for send in sends.values():
+            send.wait_send()
+    for send in relays + locals_:
         send.wait()
-    final = pltpu.make_async_copy(merged, out_ref, isem.at[0])
-    final.start()
-    final.wait()
 
 
 def per_device(estimate, views_data, psf_long, psf_short, detection):
@@ -362,23 +347,27 @@
             pltpu.VMEM((N, L), F32),
             pltpu.VMEM((N, L), F32),
             pltpu.VMEM((N, L), F32),
-            pltpu.VMEM((L, N), F32),
-            pltpu.VMEM((CHIPS, YDIM, N), F32),
-            pltpu.VMEM((CHIPS - 1, YDIM, N), F32),
-            pltpu.VMEM((L, N), F32),
+            pltpu.VMEM((CHUNKS, L, HALF), F32),
+            pltpu.VMEM((CHUNKS, CHIPS, YDIM, HALF), F32),
+            pltpu.VMEM((CHUNKS, CHIPS - 1, YDIM, HALF), F32),
+            pltpu.VMEM((CHUNKS, YDIM, HALF), F32),
             dma((5,)), dma((2,)), dma((2,)),
-            dma((CHIPS,)), dma((CHIPS,)), dma((CHIPS - 1,)), dma((CHIPS - 1,)),
-            dma((CHIPS - 1,)), dma((CHIPS - 1,)), dma((CHIPS,)), dma((CHIPS,)),
+            *[dma((CHUNKS * CHIPS,))] * 8,
         ],
         compiler_params=pltpu.CompilerParams(
-            collective_id=0, has_side_effects=True
+            collective_id=0, has_side_effects=True, vmem_limit_bytes=32 << 20
         ),
     )(
-        estimate.reshape(L, N),
-        views_data.reshape(L, N),
-        psf_long,
-        psf_short,
-        detection,
+        *(
+            pltpu.with_memory_space_constraint(a, pltpu.HBM)
+            for a in (
+                estimate.reshape(L, N),
+                views_data.reshape(L, N),
+                psf_long,
+                psf_short,
+                detection,
+            )
+        )
     )
     return estimate * factor.reshape(estimate.shape)
 

time: 55.6 us -> 53.7 us (0.966)
  other arithmetic: 1.69 us -> 0.74 us
  Pallas kernels: 53.7 us -> 52.8 us
    mul x1, other arithmetic: 1.69 us -> 0.74 us  [per_device(): return estimate * factor.reshape(estimate.shape)]
    pallas_call x1, Pallas kernels: 53.7 us -> 52.8 us  [per_device(): pl.pallas_call(kernel, out_shape=jax.ShapeDtypeStruct((L, N), F32), in_sp...]
where the time goes in v3:
time: 53.7 us; the launch traced here: 53.5 us
  Pallas kernels  52.8 us (98%)
  other arithmetic  0.74 us (1%)
    pallas_call x1, Pallas kernels, per_device(): pl.pallas_call(kernel, out_shape=jax.ShapeDtypeStruct((L, N), F32), in_sp...  52.8 us

profile of v3, /device:TPU:1, one launch (start us, length us, event | category | flops | bytes accessed | tf_op | source)
XLA Modules:
  0.0 53.5 jit_solution(10864362467078545568)
XLA Ops:
  0.0 0.0 copy-start
  0.0 52.8 %shard_map.55 = f32[128,512]{1,0:T(8,128)S(1)} custom-call(f32[128,512]{1,0:T(8,128)} %bitcast.4, f32[128,512]{1,0:T(8,128)} %bitcast.5, f32[1,61]{1,0:T(1,128)} %long_hbm.1, f32[1,2,15]{2,1,0:T(2,128)} %short_hbm.1, s32[1,2]{1,0:T(1,128)} %detect_hbm.1), custom_call_target="tpu_custom_call" | custom-call | tf_op jit(solution)/shard_map/pallas_call | solution.py:329
  52.8 0.0 copy-done
  52.8 0.7 %mul.3 = f32[8,16,512]{2,1,0:T(8,128)} multiply(f32[8,16,512]{2,1,0:T(8,128)S(1)} %copy-done, f32[8,16,512]{2,1,0:T(8,128)S(1)} %bitcast.3) | non-fusion elementwise | flops 65536 | bytes 786432 | tf_op jit(solution)/shard_map/mul | solution.py:372
Async XLA Ops:
  0.0 52.8 %copy-start = (f32[8,16,512]{2,1,0:T(8,128)S(1)}, f32[8,16,512]{2,1,0:T(8,128)}, u32[]{:S(2)}) copy-start(f32[8,16,512]{2,1,0:T(8,128)} %param.5) | copy-start | bytes 786436

commit v4 on v3

--- a/solution.py
+++ b/solution.py
@@ -76,7 +76,8 @@
 
 
 def swap_slab(x):
-    x = x.reshape(PENCILS, TILE, L)
+    rows = x.shape[0]
+    x = x.reshape(rows // TILE, TILE, L)
     sub = lax.broadcasted_iota(jnp.int32, x.shape, 1)
     lane = lax.broadcasted_iota(jnp.int32, x.shape, 2) // YDIM
     for bit in (4, 2, 1):
@@ -85,7 +86,7 @@
         up = roll(roll(x, -bit, 1), YDIM * bit, 2)
         down = up if bit == 4 else roll(roll(x, bit, 1), -YDIM * bit, 2)
         x = jnp.where(same, x, jnp.where(s_bit == 0, up, down))
-    return x.reshape(PENCILS * TILE, L)
+    return x.reshape(rows, L)
 
 
 def taps(long_ref, short_ref, detect_ref, rows):
@@ -137,6 +138,18 @@
             )
 
 
+def fill_halves(ref, blocks):
+    zero = jnp.zeros((L, L), BF16)
+    for part in range(2):
+        ref[part, 0, 0:L, 2 * L : 3 * L] = zero
+        ref[part, 1, L : 2 * L, 0:L] = zero
+    for part, value in enumerate(split(blocks)):
+        ref[part, 0, 0:L, 0 : 2 * L] = value[:, L : 3 * L]
+        ref[part, 0, L : 2 * L, :] = value
+        ref[part, 1, 0:L, :] = value
+        ref[part, 1, L : 2 * L, L : 3 * L] = value[:, 0 : 2 * L]
+
+
 HALVES = ((0, slice(L, 4 * L), slice(0, 3 * L)), (1, slice(0, 3 * L), slice(L, 4 * L)))
 
 
@@ -144,7 +157,7 @@
     est_hbm, views_hbm, long_hbm, short_hbm, detect_hbm, out_ref,
     est_ref, views_ref, long_ref, short_ref, detect_ref,
     rows, zrow, zcol, xrow, xtrow, views_t,
-    send1, recv1, send2, recv2, corr, pair, part, final,
+    send1, recv1, send2, recv2, lines, ratio, turned, corr, pair, part, final,
     isem, ssem, rsem, pair_ssem, pair_rsem, part_ssem, part_rsem,
     chip_ssem, chip_rsem, core_ssem, core_rsem,
 ):
@@ -202,30 +215,45 @@
 
     pl.semaphore_wait(barrier, PENCILS - 1 + CHIPS)
 
-    def exchange(src, dst, k):
+    def exchange(src, dst, k, far):
         mine = pl.ds(pl.multiple_of(q * TILE, TILE), TILE)
         for off in OFFSETS:
+            if off[0] != far:
+                continue
             peer = pencil(off)
             pltpu.make_async_remote_copy(
                 src_ref=src.at[pl.ds(pl.multiple_of(peer * TILE, TILE), TILE), :],
                 dst_ref=dst.at[mine, :],
-                send_sem=ssem.at[k],
-                recv_sem=rsem.at[k],
+                send_sem=ssem.at[2 * k + far],
+                recv_sem=rsem.at[2 * k + far],
                 device_id=(v, peer),
                 device_id_type=MESH,
             ).start()
-        dst[mine, :] = src[mine, :]
-
-    def arrived(src, dst, k, count):
-        span = pl.ds(0, count)
-        both = pltpu.make_async_copy(src.at[span], dst.at[span], rsem.at[k])
-        both.wait()
-        pltpu.make_async_copy(src.at[span], dst.at[span], ssem.at[k]).wait()
-
-    exchange(send1, recv1, 0)
+        if not far:
+            dst[mine, :] = src[mine, :]
+
+    def count(far):
+        return pl.ds(0, (PENCILS // 2 - 1 + far) * TILE)
+
+    def arrived(dst, k, far):
+        view = dst.at[count(far), :]
+        pltpu.make_async_copy(view, view, rsem.at[2 * k + far]).wait()
+
+    def sent(src, k):
+        for far in range(2):
+            view = src.at[count(far), :]
+            pltpu.make_async_copy(view, view, ssem.at[2 * k + far]).wait()
+
+    def half_rows(half):
+        return pl.ds(pl.multiple_of(half * 2 * L, 2 * L), 2 * L)
+
+    planes = (yh, (yh + 1) % 2)
+
+    for far in (1, 0):
+        exchange(send1, recv1, 0, far)
     xb = band_blocks(first, first_shift)
     fill_rows(xrow, xb)
-    fill_rows(
+    fill_halves(
         xtrow,
         jnp.concatenate([xb[:, k * L : (k + 1) * L].T for k in (2, 1, 0)], axis=1),
     )
@@ -233,26 +261,34 @@
     ytb = split(yb.T)
     loads[4].wait()
     views_t[...] = views_ref[...].T
-    arrived(send1, recv1, 0, (PENCILS - 1) * TILE)
-
-    gh, gl = split(swap_slab(recv1[...]))
-    ratio = []
+
+    for far in range(2):
+        arrived(recv1, 0, far)
+        rows_ = half_rows(planes[far])
+        for k, value in enumerate(split(swap_slab(recv1[rows_, :]))):
+            lines[k, rows_, :] = value
     for half, cols, window in HALVES:
         blurred = dot3(
-            (xrow[0, :, cols], xrow[1, :, cols]), (gh[window], gl[window]), NN
-        )
-        ratio.append(views_t[half * 256 : (half + 1) * 256, :] / blurred)
-    rh, rl = split(jnp.concatenate(ratio, axis=0))
-    back = jnp.concatenate(
-        [
-            dot3((xtrow[0, :, cols], xtrow[1, :, cols]), (rh[window], rl[window]), NN)
-            for _, cols, window in HALVES
-        ],
-        axis=0,
-    )
-    send2[...] = swap_slab(back)
-    exchange(send2, recv2, 1)
-    arrived(send2, recv2, 1, (PENCILS - 1) * TILE)
+            (xrow[0, :, cols], xrow[1, :, cols]),
+            (lines[0, window, :], lines[1, window, :]),
+            NN,
+        )
+        rows_ = slice(half * 2 * L, (half + 1) * 2 * L)
+        for k, value in enumerate(split(views_t[rows_, :] / blurred)):
+            ratio[k, rows_, :] = value
+    for far in (1, 0):
+        half = planes[far]
+        window = pl.ds(pl.multiple_of(half * L, L), 3 * L)
+        back = dot3(
+            (xtrow[0, half], xtrow[1, half]), (ratio[0, window, :], ratio[1, window, :]), NN
+        )
+        send2[half_rows(half), :] = swap_slab(back)
+        exchange(send2, recv2, 1, far)
+    for far in range(2):
+        arrived(recv2, 1, far)
+        part_ = dot3(ytb, split(recv2[half_rows(planes[far]), :]), NT)
+        for k, value in enumerate(split(part_)):
+            turned[k, planes[far]] = value
 
     def quarter(c, b):
         return pl.ds(pl.multiple_of((c * CHIPS + b) * YDIM, YDIM), YDIM)
@@ -271,13 +307,12 @@
 
     order = chips + [chip]
     same_core = [(b * 2 + core, q) for b in chips]
-    bh, bl = split(recv2[...].T)
+    bh, bl = (jnp.concatenate([turned[k, 0], turned[k, 1]], axis=1) for k in range(2))
     halves = {}
     for c, (_, rows_, window) in enumerate(HALVES):
-        whole = dot3(
+        corr[c] = dot3(
             (bh[:, window], bl[:, window]), (zcol[0, rows_, :], zcol[1, rows_, :]), NN
         )
-        corr[c] = dot3(ytb, split(whole), NN)
         for k, b in enumerate(order):
             halves[c, k] = remote(
                 corr.at[c, quarter(1 - core, b), :], pair.at[c, b],
@@ -316,6 +351,8 @@
             gathers[c, k].wait_recv()
             where = out_ref.at[quarter(core, chips[k]), pl.ds(c * HALF, HALF)]
             relays.append(remote(where, where, (core_ssem, core_rsem), c * CHIPS + k, partner))
+    sent(send1, 0)
+    sent(send2, 1)
     for sends in (halves, quarters, gathers):
         for send in sends.values():
             send.wait_send()
@@ -341,17 +378,20 @@
             pltpu.VMEM((2, 2 * L, 4 * L), BF16),
             pltpu.VMEM((2, 4 * L, 2 * L), BF16),
             pltpu.VMEM((2, 2 * L, 4 * L), BF16),
-            pltpu.VMEM((2, 2 * L, 4 * L), BF16),
+            pltpu.VMEM((2, 2, 2 * L, 3 * L), BF16),
             pltpu.VMEM((N, L), F32),
             pltpu.VMEM((N, L), F32),
             pltpu.VMEM((N, L), F32),
             pltpu.VMEM((N, L), F32),
             pltpu.VMEM((N, L), F32),
+            pltpu.VMEM((2, N, L), BF16),
+            pltpu.VMEM((2, N, L), BF16),
+            pltpu.VMEM((2, 2, L, 2 * L), BF16),
             pltpu.VMEM((CHUNKS, L, HALF), F32),
             pltpu.VMEM((CHUNKS, CHIPS, YDIM, HALF), F32),
             pltpu.VMEM((CHUNKS, CHIPS - 1, YDIM, HALF), F32),
             pltpu.VMEM((CHUNKS, YDIM, HALF), F32),
-            dma((5,)), dma((2,)), dma((2,)),
+            dma((5,)), dma((4,)), dma((4,)),
             *[dma((CHUNKS * CHIPS,))] * 8,
         ],
         compiler_params=pltpu.CompilerParams(

time: 53.7 us -> 53.2 us (level)
  no operation moved by 1% of the time
where the time goes in v4:
time: 53.2 us; the launch traced here: 53.1 us
  Pallas kernels  52.3 us (98%)
  other arithmetic  0.74 us (1%)
    pallas_call x1, Pallas kernels, per_device(): pl.pallas_call(kernel, out_shape=jax.ShapeDtypeStruct((L, N), F32), in_sp...  52.3 us

profile of v4, /device:TPU:1, one launch (start us, length us, event | category | flops | bytes accessed | tf_op | source)
XLA Modules:
  0.0 53.1 jit_solution(9709722558419519222)
XLA Ops:
  0.0 0.0 copy-start
  0.0 52.3 %shard_map.55 = f32[128,512]{1,0:T(8,128)S(1)} custom-call(f32[128,512]{1,0:T(8,128)} %bitcast.4, f32[128,512]{1,0:T(8,128)} %bitcast.5, f32[1,61]{1,0:T(1,128)} %long_hbm.1, f32[1,2,15]{2,1,0:T(2,128)} %short_hbm.1, s32[1,2]{1,0:T(1,128)} %detect_hbm.1), custom_call_target="tpu_custom_call" | custom-call | tf_op jit(solution)/shard_map/pallas_call | solution.py:366
  52.3 0.0 copy-done
  52.3 0.7 %mul.3 = f32[8,16,512]{2,1,0:T(8,128)} multiply(f32[8,16,512]{2,1,0:T(8,128)S(1)} %copy-done, f32[8,16,512]{2,1,0:T(8,128)S(1)} %bitcast.3) | non-fusion elementwise | flops 65536 | bytes 786432 | tf_op jit(solution)/shard_map/mul | solution.py:412
Async XLA Ops:
  0.0 52.3 %copy-start = (f32[8,16,512]{2,1,0:T(8,128)S(1)}, f32[8,16,512]{2,1,0:T(8,128)}, u32[]{:S(2)}) copy-start(f32[8,16,512]{2,1,0:T(8,128)} %param.5) | copy-start | bytes 786436

commit v5 on v4

--- a/solution.py
+++ b/solution.py
@@ -20,6 +20,7 @@
 HALF = N // CHUNKS
 L = 128
 YDIM = 16
+ROWS = L // 4
 
 NN = (((1,), (0,)), ((), ()))
 NT = (((1,), (1,)), ((), ()))
@@ -290,74 +291,124 @@
         for k, value in enumerate(split(part_)):
             turned[k, planes[far]] = value
 
-    def quarter(c, b):
-        return pl.ds(pl.multiple_of((c * CHIPS + b) * YDIM, YDIM), YDIM)
-
-    def remote(src, dst, sems, index, device):
-        send = pltpu.make_async_remote_copy(
+    outer = 1 - ((chip + 1) // 2) % 2
+    away, home = 1 - chip // 2, chip // 2
+
+    def owned(c, o):
+        return pl.ds(pl.multiple_of((c * 2 + o) * ROWS, ROWS), ROWS)
+
+    def on_chip(b):
+        return (b * 2 + core, q)
+
+    def remote(src, dst, sends, send, recvs, recv, device):
+        return pltpu.make_async_remote_copy(
             src_ref=src,
             dst_ref=dst,
-            send_sem=sems[0].at[index],
-            recv_sem=sems[1].at[index],
+            send_sem=sends.at[send],
+            recv_sem=recvs.at[recv],
             device_id=device,
             device_id_type=MESH,
         )
-        send.start()
-        return send
-
-    order = chips + [chip]
-    same_core = [(b * 2 + core, q) for b in chips]
+
+    def swap(c, k, o):
+        return remote(
+            corr.at[c, owned(1 - core, o), :], pair.at[c, o],
+            pair_ssem, 2 * c + k, pair_rsem, 2 * c + k, partner,
+        )
+
+    def collect(c, k, o, slot):
+        return remote(
+            pair.at[c, o], part.at[c, slot],
+            part_ssem, 2 * c + k, part_rsem, 3 * c + slot, on_chip(1 + o),
+        )
+
+    def place(c, o):
+        return out_ref.at[owned(core, o), pl.ds(c * HALF, HALF)]
+
+    def spread(c, k):
+        target = ((3 * (2 - chip)) % CHIPS, 3 - chip, (3 * (chip - 1)) % CHIPS)[k]
+        return remote(
+            final.at[c], place(c, home),
+            chip_ssem, 3 * c + k, chip_rsem, 2 * c + home, on_chip(target),
+        )
+
+    def landed(c, o):
+        return remote(
+            final.at[c], place(c, o), chip_ssem, 3 * c, chip_rsem, 2 * c + o, partner
+        )
+
+    def share(c, o):
+        return remote(
+            place(c, o), place(c, o), core_ssem, 2 * c + o, core_rsem, 2 * c + o, partner
+        )
+
+    def share_own(c):
+        return remote(
+            final.at[c], place(c, home),
+            core_ssem, 2 * c + home, core_rsem, 2 * c + home, partner,
+        )
+
+    def keep(c):
+        return pltpu.make_async_copy(final.at[c], place(c, home), isem.at[c])
+
     bh, bl = (jnp.concatenate([turned[k, 0], turned[k, 1]], axis=1) for k in range(2))
-    halves = {}
     for c, (_, rows_, window) in enumerate(HALVES):
         corr[c] = dot3(
             (bh[:, window], bl[:, window]), (zcol[0, rows_, :], zcol[1, rows_, :]), NN
         )
-        for k, b in enumerate(order):
-            halves[c, k] = remote(
-                corr.at[c, quarter(1 - core, b), :], pair.at[c, b],
-                (pair_ssem, pair_rsem), c * CHIPS + k, partner,
-            )
-    quarters = {}
+        for k, o in enumerate((away, home)):
+            swap(c, k, o).start()
     for c in range(CHUNKS):
-        for k, b in enumerate(order):
-            halves[c, k].wait_recv()
-            pair[c, b] = pair[c, b] * corr[c, quarter(core, b), :]
-            if k < CHIPS - 1:
-                quarters[c, k] = remote(
-                    pair.at[c, b], part.at[c, k],
-                    (part_ssem, part_rsem), c * CHIPS + k, same_core[k],
-                )
-    gathers, locals_, relays = {}, [], []
-    mine = quarter(core, chip)
+        for k, o in enumerate((away, home)):
+            swap(c, k, o).wait_recv()
+            pair[c, o] = pair[c, o] * corr[c, owned(core, o), :]
+            if k == 0:
+                collect(c, k, o, 1 - outer).start()
+            else:
+
+                @pl.when(outer == 1)
+                def _():
+                    collect(c, k, o, 2).start()
+
+    @pl.when(outer == 0)
+    def _():
+        for c in range(CHUNKS):
+            for slot in range(3):
+                collect(c, 0, home, slot).wait_recv()
+            final[c] = (pair[c, home] * part[c, 0]) * (part[c, 1] * part[c, 2])
+            for k in range(3):
+                spread(c, k).start()
+            share_own(c).start()
+            keep(c).start()
+
     for c in range(CHUNKS):
-        cols = pl.ds(c * HALF, HALF)
-        for k in range(CHIPS - 1):
-            quarters[c, k].wait_recv()
-        final[c] = (pair[c, chip] * part[c, 0]) * (part[c, 1] * part[c, 2])
-        target = out_ref.at[mine, cols]
-        for k in range(CHIPS - 1):
-            gathers[c, k] = remote(
-                final.at[c], target, (chip_ssem, chip_rsem), c * CHIPS + k, same_core[k]
-            )
-        relays.append(
-            remote(final.at[c], target, (core_ssem, core_rsem), c * CHIPS + CHIPS - 1, partner)
-        )
-        local = pltpu.make_async_copy(final.at[c], target, isem.at[c])
-        local.start()
-        locals_.append(local)
-    for c in range(CHUNKS):
-        for k in (2, 1, 0):
-            gathers[c, k].wait_recv()
-            where = out_ref.at[quarter(core, chips[k]), pl.ds(c * HALF, HALF)]
-            relays.append(remote(where, where, (core_ssem, core_rsem), c * CHIPS + k, partner))
+        landed(c, away).wait_recv()
+        share(c, away).start()
+
+        @pl.when(outer == 1)
+        def _():
+            landed(c, home).wait_recv()
+            share(c, home).start()
+
     sent(send1, 0)
     sent(send2, 1)
-    for sends in (halves, quarters, gathers):
-        for send in sends.values():
-            send.wait_send()
-    for send in relays + locals_:
-        send.wait()
+    for c in range(CHUNKS):
+        for k, o in enumerate((away, home)):
+            swap(c, k, o).wait_send()
+        collect(c, 0, away, 0).wait_send()
+
+        @pl.when(outer == 1)
+        def _():
+            collect(c, 1, home, 2).wait_send()
+
+        @pl.when(outer == 0)
+        def _():
+            for k in range(3):
+                spread(c, k).wait_send()
+            keep(c).wait()
+
+        for o in (away, home):
+            share(c, o).wait()
 
 
 def per_device(estimate, views_data, psf_long, psf_short, detection):
@@ -388,11 +439,12 @@
             pltpu.VMEM((2, N, L), BF16),
             pltpu.VMEM((2, 2, L, 2 * L), BF16),
             pltpu.VMEM((CHUNKS, L, HALF), F32),
-            pltpu.VMEM((CHUNKS, CHIPS, YDIM, HALF), F32),
-            pltpu.VMEM((CHUNKS, CHIPS - 1, YDIM, HALF), F32),
-            pltpu.VMEM((CHUNKS, YDIM, HALF), F32),
+            pltpu.VMEM((CHUNKS, 2, ROWS, HALF), F32),
+            pltpu.VMEM((CHUNKS, CHIPS - 1, ROWS, HALF), F32),
+            pltpu.VMEM((CHUNKS, ROWS, HALF), F32),
             dma((5,)), dma((4,)), dma((4,)),
-            *[dma((CHUNKS * CHIPS,))] * 8,
+            dma((CHUNKS * 2,)), dma((CHUNKS * 2,)), dma((CHUNKS * 2,)), dma((CHUNKS * 3,)),
+            dma((CHUNKS * 3,)), dma((CHUNKS * 2,)), dma((CHUNKS * 2,)), dma((CHUNKS * 2,)),
         ],
         compiler_params=pltpu.CompilerParams(
             collective_id=0, has_side_effects=True, vmem_limit_bytes=32 << 20

time: 53.2 us -> 53.3 us (level)
  no operation moved by 1% of the time
where the time goes in v5:
time: 53.3 us; the launch traced here: 53.2 us
  Pallas kernels  52.4 us (98%)
  other arithmetic  0.74 us (1%)
    pallas_call x1, Pallas kernels, per_device(): pl.pallas_call(kernel, out_shape=jax.ShapeDtypeStruct((L, N), F32), in_sp...  52.4 us

profile of v5, /device:TPU:1, one launch (start us, length us, event | category | flops | bytes accessed | tf_op | source)
XLA Modules:
  0.0 53.2 jit_solution(12048751094415088243)
XLA Ops:
  0.0 0.0 copy-start
  0.0 52.4 %shard_map.55 = f32[128,512]{1,0:T(8,128)S(1)} custom-call(f32[128,512]{1,0:T(8,128)} %bitcast.4, f32[128,512]{1,0:T(8,128)} %bitcast.5, f32[1,61]{1,0:T(1,128)} %long_hbm.1, f32[1,2,15]{2,1,0:T(2,128)} %short_hbm.1, s32[1,2]{1,0:T(1,128)} %detect_hbm.1), custom_call_target="tpu_custom_call" | custom-call | tf_op jit(solution)/shard_map/pallas_call | solution.py:417
  52.4 0.0 copy-done
  52.4 0.7 %mul.3 = f32[8,16,512]{2,1,0:T(8,128)} multiply(f32[8,16,512]{2,1,0:T(8,128)S(1)} %copy-done, f32[8,16,512]{2,1,0:T(8,128)S(1)} %bitcast.3) | non-fusion elementwise | flops 65536 | bytes 786432 | tf_op jit(solution)/shard_map/mul | solution.py:464
Async XLA Ops:
  0.0 52.4 %copy-start = (f32[8,16,512]{2,1,0:T(8,128)S(1)}, f32[8,16,512]{2,1,0:T(8,128)}, u32[]{:S(2)}) copy-start(f32[8,16,512]{2,1,0:T(8,128)} %param.5) | copy-start | bytes 786436

commit v6 on v4

--- a/solution.py
+++ b/solution.py
@@ -19,6 +19,7 @@
 CHUNKS = 2
 HALF = N // CHUNKS
 L = 128
+EDGE = 64
 YDIM = 16
 
 NN = (((1,), (0,)), ((), ()))
@@ -138,16 +139,22 @@
             )
 
 
-def fill_halves(ref, blocks):
-    zero = jnp.zeros((L, L), BF16)
-    for part in range(2):
-        ref[part, 0, 0:L, 2 * L : 3 * L] = zero
-        ref[part, 1, L : 2 * L, 0:L] = zero
-    for part, value in enumerate(split(blocks)):
-        ref[part, 0, 0:L, 0 : 2 * L] = value[:, L : 3 * L]
-        ref[part, 0, L : 2 * L, :] = value
-        ref[part, 1, 0:L, :] = value
-        ref[part, 1, L : 2 * L, L : 3 * L] = value[:, 0 : 2 * L]
+def fill_core(ref, blocks):
+    near = roll(blocks, -EDGE, 1)[:, 0 : 2 * L]
+    for part, value in enumerate(split(near)):
+        ref[part * L : (part + 1) * L, :] = value
+
+
+def store_lines(ref, rows, value):
+    hi, lo = split(value)
+    ref[rows, 0:L] = hi
+    ref[rows, L : 2 * L] = lo
+
+
+def correlate(core, lines, block):
+    window = lines[pl.ds(pl.multiple_of(block * L, L), 2 * L), :]
+    full = lax.dot_general(core[...], window, NN, preferred_element_type=F32)
+    return full[0:L, 0:L] + (full[0:L, L : 2 * L] + full[L : 2 * L, 0:L])
 
 
 HALVES = ((0, slice(L, 4 * L), slice(0, 3 * L)), (1, slice(0, 3 * L), slice(L, 4 * L)))
@@ -156,7 +163,7 @@
 def kernel(
     est_hbm, views_hbm, long_hbm, short_hbm, detect_hbm, out_ref,
     est_ref, views_ref, long_ref, short_ref, detect_ref,
-    rows, zrow, zcol, xrow, xtrow, views_t,
+    rows, zrow, zcol, xcore, xtcore, views_t,
     send1, recv1, send2, recv2, lines, ratio, turned, corr, pair, part, final,
     isem, ssem, rsem, pair_ssem, pair_rsem, part_ssem, part_rsem,
     chip_ssem, chip_rsem, core_ssem, core_rsem,
@@ -252,37 +259,41 @@
     for far in (1, 0):
         exchange(send1, recv1, 0, far)
     xb = band_blocks(first, first_shift)
-    fill_rows(xrow, xb)
-    fill_halves(
-        xtrow,
+    fill_core(xcore, xb)
+    fill_core(
+        xtcore,
         jnp.concatenate([xb[:, k * L : (k + 1) * L].T for k in (2, 1, 0)], axis=1),
     )
     fill_cols(zcol, zb)
     ytb = split(yb.T)
+    margin = jnp.zeros((EDGE, 2 * L), BF16)
+    for ref in (lines, ratio):
+        ref[0:EDGE, :] = margin
+        ref[EDGE + N :, :] = margin
     loads[4].wait()
     views_t[...] = views_ref[...].T
 
-    for far in range(2):
+    def inner(start, size):
+        return pl.ds(pl.multiple_of(EDGE + start, EDGE), size)
+
+    def arrive(far):
         arrived(recv1, 0, far)
-        rows_ = half_rows(planes[far])
-        for k, value in enumerate(split(swap_slab(recv1[rows_, :]))):
-            lines[k, rows_, :] = value
-    for half, cols, window in HALVES:
-        blurred = dot3(
-            (xrow[0, :, cols], xrow[1, :, cols]),
-            (lines[0, window, :], lines[1, window, :]),
-            NN,
-        )
-        rows_ = slice(half * 2 * L, (half + 1) * 2 * L)
-        for k, value in enumerate(split(views_t[rows_, :] / blurred)):
-            ratio[k, rows_, :] = value
+        half = planes[far]
+        store_lines(lines, inner(half * 2 * L, 2 * L), swap_slab(recv1[half_rows(half), :]))
+
+    def divide(block):
+        views = views_t[pl.ds(pl.multiple_of(block * L, L), L), :]
+        store_lines(ratio, inner(block * L, L), views / correlate(xcore, lines, block))
+
+    arrive(0)
+    divide(3 * planes[0])
+    arrive(1)
+    for block in (3 * planes[1], 1, 2):
+        divide(block)
     for far in (1, 0):
         half = planes[far]
-        window = pl.ds(pl.multiple_of(half * L, L), 3 * L)
-        back = dot3(
-            (xtrow[0, half], xtrow[1, half]), (ratio[0, window, :], ratio[1, window, :]), NN
-        )
-        send2[half_rows(half), :] = swap_slab(back)
+        back = [correlate(xtcore, ratio, 2 * half + k) for k in range(2)]
+        send2[half_rows(half), :] = swap_slab(jnp.concatenate(back, axis=0))
         exchange(send2, recv2, 1, far)
     for far in range(2):
         arrived(recv2, 1, far)
@@ -334,7 +345,8 @@
         cols = pl.ds(c * HALF, HALF)
         for k in range(CHIPS - 1):
             quarters[c, k].wait_recv()
-        final[c] = (pair[c, chip] * part[c, 0]) * (part[c, 1] * part[c, 2])
+        own = est_ref[mine, c * HALF : (c + 1) * HALF] * pair[c, chip]
+        final[c] = (own * part[c, 0]) * (part[c, 1] * part[c, 2])
         target = out_ref.at[mine, cols]
         for k in range(CHIPS - 1):
             gathers[c, k] = remote(
@@ -363,7 +375,7 @@
 def per_device(estimate, views_data, psf_long, psf_short, detection):
     raw = pl.BlockSpec(memory_space=pl.ANY)
     dma = pltpu.SemaphoreType.DMA
-    factor = pl.pallas_call(
+    updated = pl.pallas_call(
         kernel,
         out_shape=jax.ShapeDtypeStruct((L, N), F32),
         in_specs=[raw] * 5,
@@ -377,15 +389,15 @@
             pltpu.VMEM((8, L), F32),
             pltpu.VMEM((2, 2 * L, 4 * L), BF16),
             pltpu.VMEM((2, 4 * L, 2 * L), BF16),
-            pltpu.VMEM((2, 2 * L, 4 * L), BF16),
-            pltpu.VMEM((2, 2, 2 * L, 3 * L), BF16),
+            pltpu.VMEM((2 * L, 2 * L), BF16),
+            pltpu.VMEM((2 * L, 2 * L), BF16),
             pltpu.VMEM((N, L), F32),
             pltpu.VMEM((N, L), F32),
             pltpu.VMEM((N, L), F32),
             pltpu.VMEM((N, L), F32),
             pltpu.VMEM((N, L), F32),
-            pltpu.VMEM((2, N, L), BF16),
-            pltpu.VMEM((2, N, L), BF16),
+            pltpu.VMEM((N + 2 * EDGE, 2 * L), BF16),
+            pltpu.VMEM((N + 2 * EDGE, 2 * L), BF16),
             pltpu.VMEM((2, 2, L, 2 * L), BF16),
             pltpu.VMEM((CHUNKS, L, HALF), F32),
             pltpu.VMEM((CHUNKS, CHIPS, YDIM, HALF), F32),
@@ -409,7 +421,7 @@
             )
         )
     )
-    return estimate * factor.reshape(estimate.shape)
+    return updated.reshape(estimate.shape)
 
 
 def solution(mesh):

time: 53.2 us -> 52.8 us (level)
  other arithmetic: 0.74 us -> 0 us
  local copies, waits for them, and re-layouts: 0.01 us -> 0.71 us
    mul x1 -> x0, other arithmetic: 0.74 us -> none  [per_device(): return estimate * factor.reshape(estimate.shape)]
    unnamed x2 -> x1, local copies, waits for them, and re-layouts: 0.01 us -> 0.71 us
where the time goes in v6:
time: 52.8 us; the launch traced here: 52.7 us
  Pallas kernels  52 us (98%)
  local copies, waits for them, and re-layouts  0.71 us (1%)
    pallas_call x1, Pallas kernels, per_device(): pl.pallas_call(kernel, out_shape=jax.ShapeDtypeStruct((L, N), F32), in_sp...  52 us

profile of v6, /device:TPU:1, one launch (start us, length us, event | category | flops | bytes accessed | tf_op | source)
XLA Modules:
  0.0 52.7 jit_solution(16286563914227606408)
XLA Ops:
  0.0 52.0 %shard_map.55 = f32[128,512]{1,0:T(8,128)S(1)} custom-call(f32[128,512]{1,0:T(8,128)} %bitcast.4, f32[128,512]{1,0:T(8,128)} %bitcast.5, f32[1,61]{1,0:T(1,128)} %long_hbm.1, f32[1,2,15]{2,1,0:T(2,128)} %short_hbm.1, s32[1,2]{1,0:T(1,128)} %detect_hbm.1), custom_call_target="tpu_custom_call" | custom-call | tf_op jit(solution)/shard_map/pallas_call | solution.py:378
  52.0 0.7 %copy.7 = f32[8,16,512]{2,1,0:T(8,128)} copy(f32[8,16,512]{2,1,0:T(8,128)S(1)} %bitcast.3) | data formatting | bytes 524288

commit v7 on v6

--- a/solution.py
+++ b/solution.py
@@ -181,7 +181,8 @@
         pl.semaphore_signal(barrier, inc=1, device_id=(v, pencil(off)), device_id_type=MESH)
     core, chip = v % 2, v // 2
     partner = (chip * 2 + (1 - core), q)
-    chips = [(3 - chip) % CHIPS, (chip + 2) % CHIPS, (5 - chip) % CHIPS]
+    side = chip // 2
+    chips = [3 - 3 * side, 2 - side, chip + 1 - 2 * (chip % 2)]
     pl.semaphore_signal(barrier, inc=1, device_id=partner, device_id_type=MESH)
     for other in chips:
         pl.semaphore_signal(
@@ -304,17 +305,23 @@
     def quarter(c, b):
         return pl.ds(pl.multiple_of((c * CHIPS + b) * YDIM, YDIM), YDIM)
 
-    def remote(src, dst, sems, index, device):
-        send = pltpu.make_async_remote_copy(
+    def remote(src, dst, sems, k, slot, device):
+        return pltpu.make_async_remote_copy(
             src_ref=src,
             dst_ref=dst,
-            send_sem=sems[0].at[index],
-            recv_sem=sems[1].at[index],
+            send_sem=sems[0].at[k],
+            recv_sem=sems[1].at[slot],
             device_id=device,
             device_id_type=MESH,
         )
+
+    def push(*args):
+        send = remote(*args)
         send.start()
         return send
+
+    def place(c, b):
+        return out_ref.at[quarter(core, b), pl.ds(c * HALF, HALF)]
 
     order = chips + [chip]
     same_core = [(b * 2 + core, q) for b in chips]
@@ -325,9 +332,9 @@
             (bh[:, window], bl[:, window]), (zcol[0, rows_, :], zcol[1, rows_, :]), NN
         )
         for k, b in enumerate(order):
-            halves[c, k] = remote(
+            halves[c, k] = push(
                 corr.at[c, quarter(1 - core, b), :], pair.at[c, b],
-                (pair_ssem, pair_rsem), c * CHIPS + k, partner,
+                (pair_ssem, pair_rsem), c * CHIPS + k, c * CHIPS + k, partner,
             )
     quarters = {}
     for c in range(CHUNKS):
@@ -335,34 +342,46 @@
             halves[c, k].wait_recv()
             pair[c, b] = pair[c, b] * corr[c, quarter(core, b), :]
             if k < CHIPS - 1:
-                quarters[c, k] = remote(
-                    pair.at[c, b], part.at[c, k],
-                    (part_ssem, part_rsem), c * CHIPS + k, same_core[k],
+                quarters[c, k] = push(
+                    pair.at[c, b], part.at[c, chip],
+                    (part_ssem, part_rsem), c * CHIPS + k, c * CHIPS + chip, same_core[k],
                 )
     gathers, locals_, relays = {}, [], []
     mine = quarter(core, chip)
     for c in range(CHUNKS):
-        cols = pl.ds(c * HALF, HALF)
+        for b in chips:
+            remote(
+                pair.at[c, b], part.at[c, b],
+                (part_ssem, part_rsem), c * CHIPS, c * CHIPS + b, partner,
+            ).wait_recv()
+        own = est_ref[mine, c * HALF : (c + 1) * HALF] * pair[c, chip]
+        final[c] = (own * part[c, chips[0]]) * (part[c, chips[1]] * part[c, chips[2]])
         for k in range(CHIPS - 1):
-            quarters[c, k].wait_recv()
-        own = est_ref[mine, c * HALF : (c + 1) * HALF] * pair[c, chip]
-        final[c] = (own * part[c, 0]) * (part[c, 1] * part[c, 2])
-        target = out_ref.at[mine, cols]
-        for k in range(CHIPS - 1):
-            gathers[c, k] = remote(
-                final.at[c], target, (chip_ssem, chip_rsem), c * CHIPS + k, same_core[k]
+            gathers[c, k] = push(
+                final.at[c], place(c, chip),
+                (chip_ssem, chip_rsem), c * CHIPS + k, c * CHIPS + chip, same_core[k],
             )
         relays.append(
-            remote(final.at[c], target, (core_ssem, core_rsem), c * CHIPS + CHIPS - 1, partner)
-        )
-        local = pltpu.make_async_copy(final.at[c], target, isem.at[c])
+            push(
+                final.at[c], place(c, chip),
+                (core_ssem, core_rsem), c * CHIPS + chip, c * CHIPS + chip, partner,
+            )
+        )
+        local = pltpu.make_async_copy(final.at[c], place(c, chip), isem.at[c])
         local.start()
         locals_.append(local)
     for c in range(CHUNKS):
-        for k in (2, 1, 0):
-            gathers[c, k].wait_recv()
-            where = out_ref.at[quarter(core, chips[k]), pl.ds(c * HALF, HALF)]
-            relays.append(remote(where, where, (core_ssem, core_rsem), c * CHIPS + k, partner))
+        for b in (chips[2], chips[1], chips[0]):
+            remote(
+                final.at[c], place(c, b),
+                (chip_ssem, chip_rsem), c * CHIPS, c * CHIPS + b, partner,
+            ).wait_recv()
+            relays.append(
+                push(
+                    place(c, b), place(c, b),
+                    (core_ssem, core_rsem), c * CHIPS + b, c * CHIPS + b, partner,
+                )
+            )
     sent(send1, 0)
     sent(send2, 1)
     for sends in (halves, quarters, gathers):
@@ -401,7 +420,7 @@
             pltpu.VMEM((2, 2, L, 2 * L), BF16),
             pltpu.VMEM((CHUNKS, L, HALF), F32),
             pltpu.VMEM((CHUNKS, CHIPS, YDIM, HALF), F32),
-            pltpu.VMEM((CHUNKS, CHIPS - 1, YDIM, HALF), F32),
+            pltpu.VMEM((CHUNKS, CHIPS, YDIM, HALF), F32),
             pltpu.VMEM((CHUNKS, YDIM, HALF), F32),
             dma((5,)), dma((4,)), dma((4,)),
             *[dma((CHUNKS * CHIPS,))] * 8,

time: 52.8 us -> 52.7 us (level)
  no operation moved by 1% of the time
where the time goes in v7:
time: 52.7 us; the launch traced here: 52.5 us
  Pallas kernels  51.8 us (98%)
  local copies, waits for them, and re-layouts  0.71 us (1%)
    pallas_call x1, Pallas kernels, per_device(): pl.pallas_call(kernel, out_shape=jax.ShapeDtypeStruct((L, N), F32), in_sp...  51.8 us

profile of v7, /device:TPU:1, one launch (start us, length us, event | category | flops | bytes accessed | tf_op | source)
XLA Modules:
  0.0 52.5 jit_solution(1557043547731615221)
XLA Ops:
  0.0 51.8 %shard_map.55 = f32[128,512]{1,0:T(8,128)S(1)} custom-call(f32[128,512]{1,0:T(8,128)} %bitcast.4, f32[128,512]{1,0:T(8,128)} %bitcast.5, f32[1,61]{1,0:T(1,128)} %long_hbm.1, f32[1,2,15]{2,1,0:T(2,128)} %short_hbm.1, s32[1,2]{1,0:T(1,128)} %detect_hbm.1), custom_call_target="tpu_custom_call" | custom-call | tf_op jit(solution)/shard_map/pallas_call | solution.py:397
  51.8 0.7 %copy.7 = f32[8,16,512]{2,1,0:T(8,128)} copy(f32[8,16,512]{2,1,0:T(8,128)S(1)} %bitcast.3) | data formatting | bytes 524288

commit v8 on v6

--- a/solution.py
+++ b/solution.py
@@ -16,7 +16,7 @@
 PENCILS = 64
 TILE = 8
 N = 512
-CHUNKS = 2
+CHUNKS = 4
 HALF = N // CHUNKS
 L = 128
 EDGE = 64
@@ -320,15 +320,17 @@
     same_core = [(b * 2 + core, q) for b in chips]
     bh, bl = (jnp.concatenate([turned[k, 0], turned[k, 1]], axis=1) for k in range(2))
     halves = {}
-    for c, (_, rows_, window) in enumerate(HALVES):
-        corr[c] = dot3(
+    for half, rows_, window in HALVES:
+        both = dot3(
             (bh[:, window], bl[:, window]), (zcol[0, rows_, :], zcol[1, rows_, :]), NN
         )
-        for k, b in enumerate(order):
-            halves[c, k] = remote(
-                corr.at[c, quarter(1 - core, b), :], pair.at[c, b],
-                (pair_ssem, pair_rsem), c * CHIPS + k, partner,
-            )
+        for c in (2 * half, 2 * half + 1):
+            corr[c] = both[:, (c % 2) * HALF : (c % 2 + 1) * HALF]
+            for k, b in enumerate(order):
+                halves[c, k] = remote(
+                    corr.at[c, quarter(1 - core, b), :], pair.at[c, b],
+                    (pair_ssem, pair_rsem), c * CHIPS + k, partner,
+                )
     quarters = {}
     for c in range(CHUNKS):
         for k, b in enumerate(order):

time: 52.8 us -> 53.3 us (level)
  no operation moved by 1% of the time
where the time goes in v8:
time: 53.3 us; the launch traced here: 53.2 us
  Pallas kernels  52.5 us (98%)
  local copies, waits for them, and re-layouts  0.71 us (1%)
    pallas_call x1, Pallas kernels, per_device(): pl.pallas_call(kernel, out_shape=jax.ShapeDtypeStruct((L, N), F32), in_sp...  52.5 us

profile of v8, /device:TPU:1, one launch (start us, length us, event | category | flops | bytes accessed | tf_op | source)
XLA Modules:
  0.0 53.2 jit_solution(12036695758358739299)
XLA Ops:
  0.0 52.5 %shard_map.55 = f32[128,512]{1,0:T(8,128)S(1)} custom-call(f32[128,512]{1,0:T(8,128)} %bitcast.4, f32[128,512]{1,0:T(8,128)} %bitcast.5, f32[1,61]{1,0:T(1,128)} %long_hbm.1, f32[1,2,15]{2,1,0:T(2,128)} %short_hbm.1, s32[1,2]{1,0:T(1,128)} %detect_hbm.1), custom_call_target="tpu_custom_call" | custom-call | tf_op jit(solution)/shard_map/pallas_call | solution.py:380
  52.5 0.7 %copy.7 = f32[8,16,512]{2,1,0:T(8,128)} copy(f32[8,16,512]{2,1,0:T(8,128)S(1)} %bitcast.3) | data formatting | bytes 524288

commit v9 on v6

--- a/solution.py
+++ b/solution.py
@@ -16,7 +16,7 @@
 PENCILS = 64
 TILE = 8
 N = 512
-CHUNKS = 2
+CHUNKS = 1
 HALF = N // CHUNKS
 L = 128
 EDGE = 64
@@ -320,10 +320,11 @@
     same_core = [(b * 2 + core, q) for b in chips]
     bh, bl = (jnp.concatenate([turned[k, 0], turned[k, 1]], axis=1) for k in range(2))
     halves = {}
-    for c, (_, rows_, window) in enumerate(HALVES):
-        corr[c] = dot3(
+    for half, rows_, window in HALVES:
+        corr[0, :, half * 2 * L : (half + 1) * 2 * L] = dot3(
             (bh[:, window], bl[:, window]), (zcol[0, rows_, :], zcol[1, rows_, :]), NN
         )
+    for c in range(CHUNKS):
         for k, b in enumerate(order):
             halves[c, k] = remote(
                 corr.at[c, quarter(1 - core, b), :], pair.at[c, b],

time: 52.8 us -> 52.8 us (level)
  no operation moved by 1% of the time
where the time goes in v9:
time: 52.8 us; the launch traced here: 52.7 us
  Pallas kernels  52 us (98%)
  local copies, waits for them, and re-layouts  0.71 us (1%)
    pallas_call x1, Pallas kernels, per_device(): pl.pallas_call(kernel, out_shape=jax.ShapeDtypeStruct((L, N), F32), in_sp...  52 us

profile of v9, /device:TPU:1, one launch (start us, length us, event | category | flops | bytes accessed | tf_op | source)
XLA Modules:
  0.0 52.7 jit_solution(17399076455554291905)
XLA Ops:
  0.0 52.0 %shard_map.55 = f32[128,512]{1,0:T(8,128)S(1)} custom-call(f32[128,512]{1,0:T(8,128)} %bitcast.4, f32[128,512]{1,0:T(8,128)} %bitcast.5, f32[1,61]{1,0:T(1,128)} %long_hbm.1, f32[1,2,15]{2,1,0:T(2,128)} %short_hbm.1, s32[1,2]{1,0:T(1,128)} %detect_hbm.1), custom_call_target="tpu_custom_call" | custom-call | tf_op jit(solution)/shard_map/pallas_call | solution.py:379
  52.0 0.7 %copy.7 = f32[8,16,512]{2,1,0:T(8,128)} copy(f32[8,16,512]{2,1,0:T(8,128)S(1)} %bitcast.3) | data formatting | bytes 524288
